TPU v7x, 256 devices: a whole 4x4x8 slice. The times are simulated.
256 devices in a mesh: aux: 16 (over x, y), occ: 16 (over z, core).
Axes of the slice: x: 4, y: 4, z: 8, core: 2. Of those that a mesh axis runs over, the one named last changes fastest.
Arguments:
- integrals: bfloat16 [32, 384, 128, 128], P('aux', 'occ'), may hold values from -1.5 to 1.5
- coefficients: bfloat16 [4096, 384], P('occ'), may hold values from -0.21875 to 0.21875
- pair_rows: int32 [16, 384], P('aux', 'occ'), may hold values from 0 to 1
- pair_cols: int32 [16, 384], P('aux', 'occ'), may hold values from 0 to 31
- pair_count: int32 [16, 16], P('aux', 'occ'), may hold values from 1 to 24, as said below
- row_blocks: int32 [32], replicated, may hold values from 0 to 31, each once
Outputs:
- exchange_matrix: float32 [4096, 4096], P('aux', 'occ')
Inputs may be any that keep to these rules, and one draw needn't show every extreme that they name: `pair_count`: at most 24 live slots for each auxiliary block and row owner, and some auxiliary block and owner has exactly 24.
All inputs are finite; a program needn't handle non-finite values.
Results may differ from a plain program's by a relative error of at most 0.0022.
Values may be sent and summed in bfloat16 or wider, within the bound.
A program may use at most 64 MiB of HBM per device.

v0:
```python
import jax
import jax.numpy as jnp
from jax import lax
from jax.sharding import PartitionSpec as P


def contract_rows(first, second):
    return jnp.einsum("pni,pmi->nm", first, second, preferred_element_type=jnp.float32)


def local(integrals, coefficients, pair_rows, pair_cols, pair_count, row_blocks):
    aux_count = integrals.shape[0]
    block_size = integrals.shape[2]
    block_total = row_blocks.shape[0]
    occ_size = lax.axis_size("occ")
    own_blocks = block_total // occ_size
    strip_width = own_blocks * block_size
    full_coeff = lax.all_gather(coefficients, "occ", axis=0, tiled=True)
    orbitals = full_coeff.shape[1]
    coeff_blocks = full_coeff.reshape(block_total, block_size, orbitals)

    def add_pair(slot_index, partial_half):
        row_slot = pair_rows[0, slot_index]
        basis_block = row_blocks[pair_cols[0, slot_index]]
        coeff_piece = lax.dynamic_index_in_dim(coeff_blocks, basis_block, 0, keepdims=False)
        integral_piece = lax.dynamic_index_in_dim(integrals, slot_index, 1, keepdims=False)
        product = jnp.einsum(
            "pmn,ni->pmi", integral_piece, coeff_piece, preferred_element_type=jnp.float32
        )
        current = lax.dynamic_index_in_dim(partial_half, row_slot, 1, keepdims=False)
        return lax.dynamic_update_index_in_dim(partial_half, current + product, row_slot, 1)

    start_half = jnp.zeros((aux_count, own_blocks, block_size, orbitals), jnp.float32)
    summed_half = lax.fori_loop(0, pair_count[0, 0], add_pair, start_half)
    half = summed_half.reshape(aux_count, strip_width, orbitals).astype(jnp.bfloat16)
    strip = contract_rows(lax.all_gather(half, "occ", axis=1, tiled=True), half)
    summed = lax.psum(strip, "aux")
    share_rows = summed.shape[0] // lax.axis_size("aux")
    mine = lax.dynamic_slice_in_dim(summed, lax.axis_index("aux") * share_rows, share_rows, 0)
    return mine


def solution(mesh):
    return jax.shard_map(
        local,
        mesh=mesh,
        in_specs=(
            P("aux", "occ", None, None),
            P("occ", None),
            P("aux", "occ"),
            P("aux", "occ"),
            P("aux", "occ"),
            P(),
        ),
        out_specs=P("aux", "occ"),
        check_vma=False,
    )
```

profile of v0, /device:TPU:4, one launch (start us, length us, event | category | flops | bytes accessed | tf_op | source)
XLA Modules:
  0.0 470.2 jit_solution(8826988646007465637)
XLA Ops:
  7.3 45.8 %all-gather.3.cloned.1.call-done = bf16[4096,384]{1,0:T(8,128)(2,1)} async-done(((bf16[256,384]{1,0:T(8,128)(2,1)}), bf16[4096,384]{1,0:T(8,128)(2,1)}) %all-gather.3.cloned.1.call-update) | async-done | bytes 3145744 | tf_op jit(solution)/shard_map/all_gather | solution.py:18
  53.2 193.3 %while.10 = (s32[]{:T(128)}, f32[2,2,128,384]{3,2,0,1:T(8,128)S(1)}, s32[]{:T(128)}, s32[1,24]{1,0:T(1,128)}, bf16[2,24,128,128]{3,2,1,0:T(8,128)(2,1)}, /*index...) while((s32[]{:T(128)}, ...), condition=%wide.region_1.2_spmd, body=%wide.region_0.1_spmd.sunk | while | flops 25264140 | bytes 1737021 | solution.py:34
  53.8 1.3 constant_dynamic-slice_fusion.6
  59.0 1.3 dynamic_slice.46
  64.0 1.3 constant_dynamic-slice_fusion.6
  69.1 1.3 dynamic_slice.46
  74.1 1.3 constant_dynamic-slice_fusion.6
  79.3 1.3 dynamic_slice.46
  84.3 1.3 constant_dynamic-slice_fusion.6
  94.4 1.3 constant_dynamic-slice_fusion.6
  104.5 1.3 constant_dynamic-slice_fusion.6
  114.7 1.3 constant_dynamic-slice_fusion.6
  124.8 1.3 constant_dynamic-slice_fusion.6
  135.0 1.3 constant_dynamic-slice_fusion.6
  140.1 1.3 dynamic_slice.46
  145.1 1.3 constant_dynamic-slice_fusion.6
  155.2 1.3 constant_dynamic-slice_fusion.6
  165.4 1.3 constant_dynamic-slice_fusion.6
  170.5 1.3 dynamic_slice.46
  175.5 1.3 constant_dynamic-slice_fusion.6
  180.7 1.3 dynamic_slice.46
  185.7 1.3 constant_dynamic-slice_fusion.6
  195.8 1.3 constant_dynamic-slice_fusion.6
  206.0 1.3 constant_dynamic-slice_fusion.6
  211.1 1.3 dynamic_slice.46
  216.1 1.3 constant_dynamic-slice_fusion.6
  226.2 1.3 constant_dynamic-slice_fusion.6
  236.4 1.3 constant_dynamic-slice_fusion.6
  247.5 95.4 %all-gather.5.cloned.1.call-done = bf16[2,4096,384]{2,1,0:T(8,128)(2,1)} async-done(((bf16[2,256,384]{2,1,0:T(8,128)(2,1)}), bf16[2,4096,384]{2,1,0:T(8,128)(2,1)}) %all-gather.5.cloned.1.call-update) | async-done | bytes 6291472 | tf_op jit(solution)/shard_map/all_gather | solution.py:36
  342.8 6.7 %convolution_bitcast_fusion = f32[4096,256]{1,0:T(8,128)} fusion(bf16[2,4096,384]{2,1,0:T(8,128)(2,1)} %all-gather.5.cloned.1.call-done, bf16[2,256,384]{2,1,0:T(8,128)(2,1)} %bitcast.40), kind=kOutput, calls=%fused_computation.11 | convolution fusion | flops 1610612736 | bytes 10878976 | tf_op jit(solution)/shard_map/pni,pmi->nm/dot_general | solution.py:8
  349.5 112.4 %all-reduce.2.cloned.1.call-done = f32[4096,256]{1,0:T(8,128)} async-done(((f32[4096,256]{1,0:T(8,128)}), f32[4096,256]{1,0:T(8,128)}) %all-reduce.2.cloned.1.call-update) | async-done | bytes 4194320 | tf_op jit(solution)/shard_map/psum | solution.py:37
  462.0 1.7 constant_dynamic-slice_fusion.3
  (59 shorter events, 39.1 us)
Async XLA Ops:
  6.5 46.6 %all-gather.3.cloned.1.call-start = ((), (), s32[]{:S(2)}) async-start(), calls=%async_computation | async-start | bytes 3342336 | tf_op jit(solution)/shard_map/all_gather | solution.py:18
  7.3 335.6 %all-gather.5.cloned.1.call-start = ((), (), s32[]{:S(2)}) async-start(), calls=%async_computation.1 | async-start | bytes 6684672 | tf_op jit(solution)/shard_map/all_gather | solution.py:36
  247.4 214.6 %all-reduce.2.cloned.1.call-start = ((), (), s32[]{:S(2)}) async-start(), calls=%async_computation.2 | async-start | bytes 8388608 | tf_op jit(solution)/shard_map/psum | solution.py:37
Sparse Core Ops, SparseCore 0:
  9.2 43.8 all-gather.2
  247.5 95.2 all-gather.4
  349.6 112.2 all-reduce.1
where the time goes:
time: 474 us; the launch traced here: 470 us
  waiting for transfers between devices  254 us (54%)
  loops' own time  122 us (26%)
  local copies, waits for them, and re-layouts  52.2 us (11%)
  matrix products  28.3 us (6%)
  between operations  13.1 us (3%)
    another operation x1, loops' own time, local(): summed_half = lax.fori_loop(0, pair_count[0, 0], add_pair, start_half)  122 us
    psum x1, waiting for transfers between devices, local(): summed = lax.psum(strip, 'aux')  112 us
    all_gather x1, waiting for transfers between devices, local(): strip = contract_rows(lax.all_gather(half, 'occ', axis=1, tiled=True), half)  95.4 us
    dynamic_slice x38, local copies, waits for them, and re-layouts, add_pair(): basis_block = row_blocks[pair_cols[0, slot_index]]  49 us
    all_gather x1, waiting for transfers between devices, local(): full_coeff = lax.all_gather(coefficients, 'occ', axis=0, tiled=True)  45.8 us
    dot_general x19, matrix products, add_pair(): jnp.einsum('pmn,ni->pmi', integral_piece, coeff_piece, preferred_element_...  21.6 us
  transfers between devices with their start and end apart: 3, of which 3 were waited for; matrix products, arithmetic and copies ran while one was open for 0% of the time, Pallas kernels for 0%

commit v1 on v0

v1 whole, which is shorter than its diff:
```python
import jax
import jax.numpy as jnp
from jax import lax
from jax.sharding import PartitionSpec as P


def contract_rows(first, second):
    return jnp.einsum("pni,pmi->nm", first, second, preferred_element_type=jnp.float32)


def local(integrals, coefficients, pair_rows, pair_cols, pair_count, row_blocks):
    aux_count, slots, block_size, _ = integrals.shape
    block_total = row_blocks.shape[0]
    occ_size = lax.axis_size("occ")
    own_blocks = block_total // occ_size
    strip_width = own_blocks * block_size
    full_coeff = lax.all_gather(coefficients, "occ", axis=0, tiled=True)
    orbitals = full_coeff.shape[1]
    coeff_blocks = full_coeff.reshape(block_total, block_size, orbitals)

    basis_block = row_blocks[pair_cols[0]]
    gathered = jnp.take(coeff_blocks, basis_block, axis=0)
    live = jnp.arange(slots, dtype=jnp.int32) < pair_count[0, 0]
    placing = (pair_rows[0][None, :] == jnp.arange(own_blocks, dtype=jnp.int32)[:, None]) & live[None, :]
    weights = jnp.where(placing[:, :, None, None], gathered[None], jnp.zeros((), gathered.dtype))
    summed_half = jnp.einsum(
        "psmn,rsni->prmi", integrals, weights, preferred_element_type=jnp.float32
    )
    half = summed_half.reshape(aux_count, strip_width, orbitals).astype(jnp.bfloat16)
    strip = contract_rows(lax.all_gather(half, "occ", axis=1, tiled=True), half)
    return lax.psum_scatter(strip, "aux", scatter_dimension=0, tiled=True)


def solution(mesh):
    return jax.shard_map(
        local,
        mesh=mesh,
        in_specs=(
            P("aux", "occ", None, None),
            P("occ", None),
            P("aux", "occ"),
            P("aux", "occ"),
            P("aux", "occ"),
            P(),
        ),
        out_specs=P("aux", "occ"),
        check_vma=False,
    )
```

time: 474 us -> 201 us (0.42)
  loops' own time: 122 us -> 0 us
  waiting for transfers between devices: 254 us -> 169 us
  local copies, waits for them, and re-layouts: 52.2 us -> 6.52 us
  matrix products: 28.3 us -> 8.14 us
    another operation x1 -> x0, loops' own time: 122 us -> none  [local(): summed_half = lax.fori_loop(0, pair_count[0, 0], add_pair, start_half)]
    psum x1 -> x0, waiting for transfers between devices: 112 us -> none  [local(): summed = lax.psum(strip, 'aux')]
    reduce_scatter x0 -> x1, waiting for transfers between devices: none -> 81 us  [local(): return lax.psum_scatter(strip, 'aux', scatter_dimension=0, tiled=True)]
    dynamic_slice x58 -> x0, local copies, waits for them, and re-layouts: 51.3 us -> none  [the longest x38 49 us: add_pair(): basis_block = row_blocks[pair_cols[0, slot_index]]]
    all_gather x1, waiting for transfers between devices: 95.4 us -> 44.8 us  [local(): strip = contract_rows(lax.all_gather(half, 'occ', axis=1, tiled=True), half)]
    dot_general x19 -> x1, matrix products: 21.6 us -> 1.47 us  [local(): jnp.einsum('psmn,rsni->prmi', integrals, weights, preferred_element_type=...]
    gather x0 -> x2, local copies, waits for them, and re-layouts: none -> 5.7 us  [the longest x1 4.35 us: local(): gathered = jnp.take(coeff_blocks, basis_block, axis=0)]
  transfers between devices with their start and end apart: 3 -> 3, of which waited for: 3 -> 3; matrix products, arithmetic and copies ran while one was open for 0% -> 1% of each run, Pallas kernels for 0% -> 0%
where the time goes in v1:
time: 201 us
  waiting for transfers between devices  169 us (84%)
  between operations  13.8 us (7%)
  matrix products  8.14 us (4%)
  local copies, waits for them, and re-layouts  6.52 us (3%)
  other arithmetic  3.35 us (2%)
    reduce_scatter x1, waiting for transfers between devices, local(): return lax.psum_scatter(strip, 'aux', scatter_dimension=0, tiled=True)  81 us
    all_gather x1, waiting for transfers between devices, local(): strip = contract_rows(lax.all_gather(half, 'occ', axis=1, tiled=True), half)  44.8 us
    all_gather x1, waiting for transfers between devices, local(): full_coeff = lax.all_gather(coefficients, 'occ', axis=0, tiled=True)  42.4 us
    dot_general x1, matrix products, contract_rows(): jnp.einsum('pni,pmi->nm', first, second, preferred_element_type=jnp.float32)  6.67 us
    gather x1, local copies, waits for them, and re-layouts, local(): gathered = jnp.take(coeff_blocks, basis_block, axis=0)  4.35 us
  transfers between devices with their start and end apart: 3, of which 3 were waited for; matrix products, arithmetic and copies ran while one was open for 1% of the time, Pallas kernels for 0%

profile of v1, /device:TPU:4, one launch (start us, length us, event | category | flops | bytes accessed | tf_op | source)
XLA Modules:
  0.0 200.9 jit_solution(10329253605268713100)
XLA Ops:
  6.5 0.0 copy-start
  6.5 0.0 all-gather.3.cloned.1.call-start
  6.5 0.7 all-gather.3.cloned.1.call-update
  7.3 0.0 all-gather.5.cloned.1.call-start
  8.0 0.7 fusion.22
  8.6 1.4 gather_fusion
  10.0 0.7 compare_and_fusion.1
  10.7 42.4 %all-gather.3.cloned.1.call-done = bf16[4096,384]{1,0:T(8,128)(2,1)} async-done(((bf16[256,384]{1,0:T(8,128)(2,1)}), bf16[4096,384]{1,0:T(8,128)(2,1)}) %all-gather.3.cloned.1.call-update) | async-done | bytes 3145744 | tf_op jit(solution)/shard_map/all_gather | solution.py:17
  53.1 4.4 %gather_fusion.1 = bf16[24,128,384]{2,1,0:T(8,128)(2,1)} fusion(bf16[32,128,384]{2,1,0:T(8,128)(2,1)} %bitcast.48, s32[1024]{0:T(1024)S(1)} %pad_clamp_fusion), kind=kCustom, calls=%fused_computation.1 | custom fusion | bytes 4718688 | tf_op jit(solution)/shard_map/jit(_take)/gather | solution.py:22
  57.5 2.0 broadcast_select_fusion
  59.5 0.0 copy-done
  59.5 1.5 fusion.17
  61.0 0.8 copy.7
  61.8 0.0 all-gather.5.cloned.1.call-update
  61.8 0.0 reduce-scatter.2.cloned.1.call-start
  61.9 44.8 %all-gather.5.cloned.1.call-done = bf16[2,4096,384]{2,1,0:T(8,128)(2,1)} async-done(((bf16[2,256,384]{2,1,0:T(8,128)(2,1)}), bf16[2,4096,384]{2,1,0:T(8,128)(2,1)}) %all-gather.5.cloned.1.call-update) | async-done | bytes 6291472 | tf_op jit(solution)/shard_map/all_gather | solution.py:30
  106.6 6.7 %convolution_bitcast_fusion = f32[4096,256]{1,0:T(8,128)} fusion(bf16[2,4096,384]{2,1,0:T(8,128)(2,1)} %all-gather.5.cloned.1.call-done, bf16[2,256,384]{2,1,0:T(8,128)(2,1)} %bitcast.47), kind=kOutput, calls=%fused_computation.2 | convolution fusion | flops 1610612736 | bytes 10878976 | tf_op jit(solution)/shard_map/pni,pmi->nm/dot_general | solution.py:8
  113.3 0.0 reduce-scatter.2.cloned.1.call-update
  113.3 81.0 %reduce-scatter.2.cloned.1.call-done = f32[256,256]{1,0:T(8,128)} async-done(((f32[4096,256]{1,0:T(8,128)}), f32[256,256]{1,0:T(8,128)}) %reduce-scatter.2.cloned.1.call-update) | async-done | bytes 262160 | tf_op jit(solution)/shard_map/reduce_scatter | solution.py:31
  (5 shorter events, 0.0 us)
Async XLA Ops:
  6.5 52.9 %copy-start = (bf16[2,24,128,128]{3,2,1,0:T(8,128)(2,1)S(1)}, bf16[2,24,128,128]{3,2,1,0:T(8,128)(2,1)}, u32[]{:S(2)}) copy-start(bf16[2,24,128,128]{3,2,1,0:T(8,128)(2,1)} %param.6) | copy-start | bytes 4718596
  6.5 46.6 %all-gather.3.cloned.1.call-start = ((), (), s32[]{:S(2)}) async-start(), calls=%async_computation.1 | async-start | bytes 3342336 | tf_op jit(solution)/shard_map/all_gather | solution.py:17
  7.3 99.4 %all-gather.5.cloned.1.call-start = ((), (), s32[]{:S(2)}) async-start(), calls=%async_computation.2 | async-start | bytes 6684672 | tf_op jit(solution)/shard_map/all_gather | solution.py:30
  61.8 132.5 %reduce-scatter.2.cloned.1.call-start = ((), (), s32[]{:S(2)}) async-start(), calls=%async_computation.3 | async-start | bytes 4456448 | tf_op jit(solution)/shard_map/reduce_scatter | solution.py:31
Sparse Core Ops, SparseCore 0:
  9.2 43.8 all-gather.2
  61.9 44.6 all-gather.4
  113.4 80.8 reduce-scatter.1
